TPU v7x, 256 devices: a whole 4x4x8 slice. The times are simulated.
256 devices in a mesh: section: 16 (over y, z_lo), dp: 8 (over z_hi, x), tensor: 2 (over core).
Axes of the slice: x: 4, y: 4, z: 8 (z_hi: 2, z_lo: 4; z = z_hi * 4 + z_lo), core: 2. Of those that a mesh axis runs over, the one named last changes fastest.
Arguments:
- context: bfloat16 [16, 16, 256, 2048], P('section', 'dp'), may hold values from -6 to 6
- queries: bfloat16 [16, 16, 64, 2048], P('section', 'dp'), may hold values from -6 to 6
- lengths: int32 [16, 16], P('section', 'dp'), may hold values from 32 to 256
- norm_gain: float32 [16, 2048], P('section'), may hold values from 0.1 to 1.9
- qkv_weight: bfloat16 [16, 2048, 3, 2048], P('section', 'dp', None, 'tensor')
- out_weight: bfloat16 [16, 2048, 2048], P('section', 'tensor', 'dp'), may hold values from -0.5 to 0.5
Outputs:
- next_context: bfloat16 [16, 16, 256, 2048], P('section', 'dp')
- next_queries: bfloat16 [16, 16, 64, 2048], P('section', 'dp')
All inputs are finite; a program needn't handle non-finite values.
Results may differ from a plain program's by a relative error of at most 0.014.
The roundings to bfloat16 on the way count: a program that leaves them out, or rounds other values in their place, can miss the bound.
Values may be sent and summed in bfloat16 or wider, within the bound.
No kernel may reach another device: no remote copies, remote signals or barrier semaphores. Data moves between devices by JAX's collectives and lax.ppermute only.
A program may use at most 128 MiB of HBM per device.

v0:
```python
import math

import jax
import jax.numpy as jnp
from jax import lax
from jax.sharding import PartitionSpec as P

HEAD = 128


def from_behind(array, axis, by):
    count = lax.axis_size(axis)
    return lax.ppermute(array, axis, [(i, (i + by) % count) for i in range(count)])


def attend(projected, valid_len, first_row, row_count, memory_rows):
    query_part = projected[:, first_row : first_row + row_count, 0]
    key_part = projected[:, :memory_rows, 1]
    value_part = projected[:, :memory_rows, 2]
    scores = jnp.einsum(
        "brhd,bjhd->bhrj", query_part, key_part, preferred_element_type=jnp.float32
    ) * (1.0 / math.sqrt(HEAD))
    key_index = jnp.arange(memory_rows, dtype=jnp.int32)
    valid = key_index[None, None, None, :] < valid_len[:, None, None, None]
    scores = jnp.where(valid, scores, -1e30)
    top_score = jnp.max(scores, axis=-1, keepdims=True)
    expo = jnp.exp(scores - top_score)
    probs = (expo / jnp.sum(expo, axis=-1, keepdims=True)).astype(jnp.bfloat16)
    mixed = jnp.einsum(
        "bhrj,bjhd->brhd", probs, value_part, preferred_element_type=jnp.float32
    ).astype(jnp.bfloat16)
    return mixed


def per_device(context, queries, lengths, norm_gain, qkv_weight, out_weight):
    context_rows = context[0]
    query_rows = queries[0]
    stream_rows = jnp.concatenate([context_rows, query_rows], axis=1)
    scene_count = stream_rows.shape[0]
    row_total = stream_rows.shape[1]
    model_width = stream_rows.shape[2]
    memory_rows = context.shape[2]
    local_width = qkv_weight.shape[3]
    head_count = local_width // HEAD
    encoder_flag = lax.axis_index("section") < lax.axis_size("section") // 2
    widened = stream_rows.astype(jnp.float32)
    mean_square = jnp.mean(widened * widened, axis=-1, keepdims=True)
    normed = (widened * lax.rsqrt(mean_square + 1e-06) * norm_gain[0]).astype(jnp.bfloat16)
    flat_rows = normed.reshape(scene_count * row_total, model_width)
    weight_rows = lax.all_gather(qkv_weight, "dp", axis=1, tiled=True)
    row_count = weight_rows.shape[1]
    projected = jnp.dot(
        flat_rows,
        weight_rows[0].reshape(row_count, 3 * local_width),
        preferred_element_type=jnp.float32,
    )
    projected = projected.astype(jnp.bfloat16).reshape(scene_count, row_total, 3, head_count, HEAD)
    mixed = attend(projected, lengths[0], 0, row_total, memory_rows)
    row_index = jnp.arange(row_total, dtype=jnp.int32)
    keep_rows = jnp.where(encoder_flag, row_index < memory_rows, row_index >= memory_rows)
    mixed = mixed * keep_rows[None, :, None, None].astype(jnp.bfloat16)
    mixed_flat = mixed.reshape(scene_count * row_total, local_width)
    update = jnp.dot(
        mixed_flat,
        lax.all_gather(out_weight, "dp", axis=2, tiled=True)[0],
        preferred_element_type=jnp.float32,
    )
    update = update.reshape(scene_count, row_total, model_width)
    head_total = lax.psum(update.astype(jnp.bfloat16), "tensor").astype(jnp.float32)
    fresh = (widened + head_total).astype(jnp.bfloat16)
    context_new = fresh[:, :memory_rows]
    query_new = fresh[:, memory_rows:]
    passed = from_behind((context_new, query_new), "section", 1)
    return (passed[0][None], passed[1][None])


def solution(mesh):
    return jax.shard_map(
        per_device,
        mesh=mesh,
        in_specs=(
            P("section", "dp", None, None),
            P("section", "dp", None, None),
            P("section", "dp"),
            P("section", None),
            P("section", "dp", None, "tensor"),
            P("section", "tensor", "dp"),
        ),
        out_specs=(P("section", "dp", None, None), P("section", "dp", None, None)),
        check_vma=False,
    )
```

profile of v0, /device:TPU:17, one launch (start us, length us, event | category | flops | bytes accessed | tf_op | source)
XLA Modules:
  0.0 486.5 jit_solution(638077608019087004)
XLA Ops:
  7.2 0.0 copy-start
  7.2 0.0 copy-start.1
  7.2 0.0 copy-start.3
  7.2 0.0 copy-start.2
  7.2 0.0 all-gather.3.cloned.1.call-start
  7.3 2.7 copy.11
  10.0 0.0 all-gather.3.cloned.1.call-update
  10.0 0.0 all-gather.5.cloned.1.call-start
  10.1 0.7 all-gather.5.cloned.1.call-update
  10.8 0.0 all-reduce.2.cloned.1.call-start
  10.8 0.0 copy-done
  10.8 0.0 copy-done.1
  10.8 0.6 fusion.1
  11.4 0.0 copy-done.3
  11.4 0.1 iota_compare_fusion.2
  11.5 0.0 copy-done.2
  11.5 2.2 fusion.3
  13.7 253.5 %all-gather.3.cloned.1.call-done = bf16[1,2048,3,1024]{1,3,2,0:T(8,128)(2,1)} async-done(((bf16[1,256,3,1024]{1,3,2,0:T(8,128)(2,1)}), bf16[1,2048,3,1024]{1,3,2,0:T(8,128)(2,1)}) %all-gather.3.cloned.1.call-update) | async-done | bytes 12582928 | tf_op jit(solution)/shard_map/all_gather | solution.py:50
  267.2 12.1 %fusion.15 = bf16[80,8,24,128]{3,1,2,0:T(8,128)(2,1)S(1)} fusion(bf16[640,2048]{1,0:T(8,128)(2,1)} %bitcast.43, bf16[2048,3072]{0,1:T(8,128)(2,1)} %bitcast.47), kind=kOutput, calls=%fused_computation.21 | convolution fusion | flops 8055029760 | bytes 19136512 | tf_op jit(solution)/shard_map/dot_general | solution.py:52
  279.3 1.1 copy.20
  280.4 0.1 slice.20
  280.5 0.4 fusion.24
  280.9 0.9 fusion.19
  281.8 2.4 fusion.25
  284.2 2.0 multiply_bitcast_fusion
  286.2 90.6 %all-gather.5.cloned.1.call-done = bf16[1,1024,2048]{2,1,0:T(8,128)(2,1)} async-done(((bf16[1,1024,256]{2,1,0:T(8,128)(2,1)}), bf16[1,1024,2048]{2,1,0:T(8,128)(2,1)}) %all-gather.5.cloned.1.call-update) | async-done | bytes 4194320 | tf_op jit(solution)/shard_map/all_gather | solution.py:65
  376.7 7.0 %fusion.8 = bf16[2,320,2048]{2,1,0:T(8,128)(2,1)} fusion(bf16[1,1024,2048]{2,1,0:T(8,128)(2,1)} %all-gather.5.cloned.1.call-done, bf16[2,8,40,8,128]{4,3,2,1,0:T(8,128)(2,1)} %multiply_bitcast_fusion), kind=kOutput, calls=%fused_computation.15 | convolution fusion | flops 2685665280 | bytes 8126464 | tf_op jit(solution)/shard_map/dot_general | solution.py:63
  383.7 0.0 all-reduce.2.cloned.1.call-update
  383.7 30.2 %all-reduce.2.cloned.1.call-done = bf16[2,320,2048]{2,1,0:T(8,128)(2,1)} async-done(((bf16[2,320,2048]{2,1,0:T(8,128)(2,1)}), bf16[2,320,2048]{2,1,0:T(8,128)(2,1)}) %all-reduce.2.cloned.1.call-update) | async-done | bytes 2621456 | tf_op jit(solution)/shard_map/psum | solution.py:69
  413.9 2.8 fusion.4
  416.7 0.1 slice.23
  416.9 1.4 collective-permute-start
  418.3 1.4 collective-permute-start.1
  419.6 58.3 %collective-permute-done.1 = bf16[2,64,2048]{2,1,0:T(8,128)(2,1)S(1)} collective-permute-done((bf16[2,64,2048]{2,1,0:T(8,128)(2,1)S(1)}, bf16[2,64,2048]{2,1,0:T(8,128)(2,1)S(1)}, u32[]{:S(2)}, u32[]{:S(2)}) %collective-permute-start.1) | collective-permute-done | bytes 524320 | tf_op jit(solution)/shard_map/ppermute | solution.py:13
  477.9 0.0 collective-permute-done
  477.9 1.3 copy.34
  479.2 0.8 copy.35
  (3 shorter events, 0.0 us)
Async XLA Ops:
  7.2 3.7 copy-start
  7.2 3.7 copy-start.1
  7.2 4.3 copy-start.3
  7.2 4.3 copy-start.2
  7.2 260.0 %all-gather.3.cloned.1.call-start = ((), (), s32[]{:S(2)}) async-start(), calls=%async_computation | async-start | bytes 14155776 | tf_op jit(solution)/shard_map/all_gather | solution.py:50
  10.0 366.7 %all-gather.5.cloned.1.call-start = ((), (), s32[]{:S(2)}) async-start(), calls=%async_computation.1 | async-start | bytes 4718592 | tf_op jit(solution)/shard_map/all_gather | solution.py:65
  10.8 403.2 %all-reduce.2.cloned.1.call-start = ((), (), s32[]{:S(2)}) async-start(), calls=%async_computation.2 | async-start | bytes 5242880 | tf_op jit(solution)/shard_map/psum | solution.py:69
  416.9 61.0 %collective-permute-start = (bf16[2,256,2048]{2,1,0:T(8,128)(2,1)S(1)}, bf16[2,256,2048]{2,1,0:T(8,128)(2,1)S(1)}, u32[]{:S(2)}, u32[]{:S(2)}) collective-permute-start(bf16[2,256,2048]{2,1,0:T(8,128)(2,1)S(1)} %slice.23), channel_id=1, source_target_pairs={{0,16},{16,32},{32,48},{48,64},{64,80},{80,96},{96,112},{112,128},... | collective-permute-start | bytes 6291464 | tf_op jit(solution)/shard_map/ppermute | solution.py:13
  418.3 59.6 %collective-permute-start.1 = (bf16[2,64,2048]{2,1,0:T(8,128)(2,1)S(1)}, bf16[2,64,2048]{2,1,0:T(8,128)(2,1)S(1)}, u32[]{:S(2)}, u32[]{:S(2)}) collective-permute-start(bf16[2,64,2048]{2,1,0:T(8,128)(2,1)S(1)} %slice.24), channel_id=1, source_target_pairs={{0,16},{16,32},{32,48},{48,64},{64,80},{80,96},{96,112},{112,128},... | collective-permute-start | bytes 1572872 | tf_op jit(solution)/shard_map/ppermute | solution.py:13
Sparse Core Ops, SparseCore 0:
  11.1 256.0 all-gather.2
  269.7 107.0 all-gather.4
  383.9 30.0 all-reduce.1
where the time goes:
time: 489 us; the launch traced here: 487 us
  waiting for transfers between devices  433 us (89%)
  matrix products  21.9 us (4%)
  between operations  13.9 us (3%)
  other arithmetic  8.03 us (2%)
  local copies, waits for them, and re-layouts  6.61 us (1%)
    all_gather x1, waiting for transfers between devices, per_device(): weight_rows = lax.all_gather(qkv_weight, 'dp', axis=1, tiled=True)  253 us
    all_gather x1, waiting for transfers between devices, per_device(): lax.all_gather(out_weight, 'dp', axis=2, tiled=True)[0]  90.6 us
    ppermute x2, waiting for transfers between devices, from_behind(): lax.ppermute(array, axis, [(i, (i + by) % count) for i in range(count)])  58.3 us
    psum x1, waiting for transfers between devices, per_device(): lax.psum(update.astype(jnp.bfloat16), 'tensor').astype(jnp.float32)  30.2 us
    dot_general x1, matrix products, per_device(): jnp.dot(flat_rows, weight_rows[0].reshape(row_count, 3 * local_width), pr...  12.1 us
  transfers between devices with their start and end apart: 5, of which 4 were waited for; matrix products, arithmetic and copies ran while one was open for 4% of the time, Pallas kernels for 0%

commit v1 on v0

v1 whole, which is shorter than its diff:
```python
import functools
import math

import jax
import jax.numpy as jnp
from jax import lax
from jax.experimental import pallas as pl
from jax.experimental.pallas import tpu as pltpu
from jax.sharding import PartitionSpec as P

HEAD = 128
RING = 4
VMEM_LIMIT = 56 * 1024 * 1024
ANY = pl.BlockSpec(memory_space=pl.ANY)
SMEM = pl.BlockSpec(memory_space=pltpu.SMEM)
VMEM = pl.BlockSpec(memory_space=pltpu.VMEM)
BF16 = jnp.bfloat16
F32 = jnp.float32


def around_x(array, by, sections=None):
    pairs = [
        (z * RING + x, z * RING + (x + by) % RING) for z in range(2) for x in range(RING)
    ]
    return lax.ppermute(array, "dp", pairs)


def around_x_of(array, by, sections):
    pairs = []
    for s in sections:
        for z in range(2):
            for x in range(RING):
                base = s * 2 * RING + z * RING
                pairs.append((base + x, base + (x + by) % RING))
    return lax.ppermute(array, ("section", "dp"), pairs)


def across_z(array):
    return lax.ppermute(array, "dp", [(d, (d + RING) % (2 * RING)) for d in range(2 * RING)])


def other_core(array):
    return lax.ppermute(array, "tensor", [(0, 1), (1, 0)])


def relay(array, sections, count):
    return lax.ppermute(array, "section", [(s, (s + 1) % count) for s in sections])


def after(array, *others):
    return lax.optimization_barrier((array,) + others)[0]


def copy_all(copies):
    for copy in copies:
        copy.start()
    return copies


def wait_all(copies):
    for copy in copies:
        copy.wait()


def call(kernel, outs, in_specs, out_specs, scratch=(), flops=0, moved=0):
    return pl.pallas_call(
        kernel,
        out_shape=outs,
        in_specs=in_specs,
        out_specs=out_specs,
        scratch_shapes=list(scratch),
        compiler_params=pltpu.CompilerParams(vmem_limit_bytes=VMEM_LIMIT),
        cost_estimate=pl.CostEstimate(flops=flops, bytes_accessed=moved, transcendentals=0),
    )


def quarter_kernel(where, weight, *pieces):
    x = where[0]
    width = pieces[0].shape[2]
    for step, piece in enumerate(pieces):
        start = pl.multiple_of(((x + step) % RING) * width, width)
        piece[...] = weight[:, :, pl.ds(start, width)]


def quarters(where, weight):
    planes, rows, columns = weight.shape
    piece = jax.ShapeDtypeStruct((planes, rows, columns // RING), BF16)
    return call(
        quarter_kernel, (piece,) * RING, [SMEM, VMEM], (VMEM,) * RING, moved=4 * weight.size
    )(where, weight)


def norm_kernel(where, context, queries, gain, ctx_out, qry_out, ctx_norm, qry_norm, *scratch):
    ctx, qry, sems = scratch
    core = where[3]
    copies = copy_all(
        [
            pltpu.make_async_copy(context.at[core], ctx, sems.at[0]),
            pltpu.make_async_copy(queries.at[core], qry, sems.at[1]),
        ]
    )
    step = 32

    def rows_of(source, raw, target):
        @pl.loop(0, source.shape[0] // step)
        def _(i):
            at = pl.ds(pl.multiple_of(i * step, step), step)
            low = source[at, :]
            wide = low.astype(F32)
            mean = jnp.mean(wide * wide, axis=-1, keepdims=True)
            target[at, :] = (wide * lax.rsqrt(mean + 1e-06) * gain[...]).astype(BF16)
            raw[at, :] = low

    copies[0].wait()
    rows_of(ctx, ctx_out, ctx_norm)
    copies[1].wait()
    rows_of(qry, qry_out, qry_norm)


def norm_scene(where, context, queries, gain):
    ctx = jax.ShapeDtypeStruct(context.shape[1:], BF16)
    qry = jax.ShapeDtypeStruct(queries.shape[1:], BF16)
    return call(
        norm_kernel,
        (ctx, qry, ctx, qry),
        [SMEM, ANY, ANY, VMEM],
        (VMEM,) * 4,
        [
            pltpu.VMEM(ctx.shape, BF16),
            pltpu.VMEM(qry.shape, BF16),
            pltpu.SemaphoreType.DMA((2,)),
        ],
        moved=6 * ctx.size,
    )(where, context, queries, gain)


def attend_kernel(where, lengths, *refs):
    ctx = refs[:5]
    qry = refs[5:9]
    near = refs[9:17]
    far = refs[17:25]
    outs = refs[25:29]
    rows_all, qry_all, weight, q_buf, k_buf, v_buf, mixed, sems = refs[29:]
    x, z, encoder = where[0], where[1], where[2]
    mem = rows_all.shape[1]
    few = qry_all.shape[1]
    part = near[0].shape[2]
    block = near[0].shape[1]
    half = mem // 2
    copies = [
        pltpu.make_async_copy(ctx[0], rows_all.at[0], sems.at[0]),
        pltpu.make_async_copy(ctx[1], rows_all.at[1], sems.at[1]),
        pltpu.make_async_copy(ctx[2], rows_all.at[2, pl.ds(0, half)], sems.at[2]),
        pltpu.make_async_copy(ctx[3], rows_all.at[2, pl.ds(half, half)], sems.at[3]),
        pltpu.make_async_copy(ctx[4], rows_all.at[3], sems.at[4]),
    ]
    for slot in range(RING):
        copies.append(pltpu.make_async_copy(qry[slot], qry_all.at[slot], sems.at[5 + slot]))
    for side, (group, high) in enumerate(((near, z), (far, 1 - z))):
        for step in range(RING):
            first = (high * RING + (x - step + RING) % RING) * block
            first = pl.multiple_of(first, block)
            for side_core in range(2):
                copies.append(
                    pltpu.make_async_copy(
                        group[side_core * RING + step],
                        weight.at[:, pl.ds(first, block), pl.ds(side_core * part, part)],
                        sems.at[9 + side * 8 + step * 2 + side_core],
                    )
                )
    copy_all(copies)
    wait_all(copies)
    heads = 2 * part // HEAD
    scale = 1.0 / math.sqrt(HEAD)
    column = lax.broadcasted_iota(jnp.int32, (mem, mem), 1)

    @pl.loop(0, RING)
    def _(slot):
        rows = rows_all[slot]

        @pl.when(encoder == 1)
        def _():
            q_buf[...] = jnp.dot(rows, weight[0], preferred_element_type=F32).astype(BF16)

        @pl.when(encoder == 0)
        def _():
            q_buf[...] = jnp.zeros_like(q_buf)
            q_buf[pl.ds(0, few), :] = jnp.dot(
                qry_all[slot], weight[0], preferred_element_type=F32
            ).astype(BF16)

        k_buf[...] = jnp.dot(rows, weight[1], preferred_element_type=F32).astype(BF16)
        v_buf[...] = jnp.dot(rows, weight[2], preferred_element_type=F32).astype(BF16)
        valid = column < lengths[slot]
        for head in range(heads):
            at = pl.ds(head * HEAD, HEAD)
            scores = (
                lax.dot_general(
                    q_buf[:, at],
                    k_buf[:, at],
                    (((1,), (1,)), ((), ())),
                    preferred_element_type=F32,
                )
                * scale
            )
            scores = jnp.where(valid, scores, -1e30)
            expo = jnp.exp(scores - jnp.max(scores, axis=-1, keepdims=True))
            probs = (expo / jnp.sum(expo, axis=-1, keepdims=True)).astype(BF16)
            mixed[slot, :, at] = jnp.dot(
                probs, v_buf[:, at], preferred_element_type=F32
            ).astype(BF16)

    wait_all(
        copy_all(
            [
                pltpu.make_async_copy(mixed.at[slot], outs[slot], sems.at[slot])
                for slot in range(RING)
            ]
        )
    )


def attend(where, lengths, ctx, qry, near, far):
    mem, width = ctx[0].shape
    few = qry[0].shape[0]
    planes, block, part = near[0].shape
    out = jax.ShapeDtypeStruct((mem, 2 * part), BF16)
    operands = (*ctx, *qry, *near, *far)
    return call(
        attend_kernel,
        (out,) * RING,
        [SMEM, SMEM] + [ANY] * len(operands),
        (ANY,) * RING,
        [
            pltpu.VMEM((RING, mem, width), BF16),
            pltpu.VMEM((RING, few, width), BF16),
            pltpu.VMEM((planes, width, 2 * part), BF16),
            pltpu.VMEM((mem, 2 * part), BF16),
            pltpu.VMEM((mem, 2 * part), BF16),
            pltpu.VMEM((mem, 2 * part), BF16),
            pltpu.VMEM((RING, mem, 2 * part), BF16),
            pltpu.SemaphoreType.DMA((25,)),
        ],
        flops=2 * RING * mem * width * planes * 2 * part,
        moved=2 * (RING * mem * width + planes * width * 2 * part),
    )(where, lengths, *operands)


def project_kernel(crossed, where, context, queries, *refs):
    mixed = refs[:4]
    weights = refs[4:12]
    out = refs[12]
    heads, weight, base, sems = refs[13:]
    x, z, encoder, core = where[0], where[1], where[2], where[3]
    part = mixed[0].shape[1] // 2
    inner, block = weights[0].shape
    half = (1 - z) if crossed else z
    first = pl.multiple_of(half * RING * block, RING * block)
    few = queries.shape[1]

    @pl.when(encoder == 1)
    def _():
        pltpu.make_async_copy(
            context.at[core, :, pl.ds(first, RING * block)], base, sems.at[0]
        ).start()

    @pl.when(encoder == 0)
    def _():
        pltpu.make_async_copy(
            queries.at[core, :, pl.ds(first, RING * block)],
            base.at[pl.ds(0, few)],
            sems.at[0],
        ).start()

    copies = []
    for step in range(RING):
        for side in range(2):
            at = pl.multiple_of(side * inner + ((x + step) % RING) * part, part)
            copies.append(
                pltpu.make_async_copy(
                    mixed[step].at[:, pl.ds(side * part, part)],
                    heads.at[:, pl.ds(at, part)],
                    sems.at[1 + step * 2 + side],
                )
            )
    pieces = []
    for step in range(RING):
        for side in range(2):
            pieces.append(
                pltpu.make_async_copy(
                    weights[side * RING + step],
                    weight.at[step, pl.ds(side * inner, inner)],
                    sems.at[9 + step * 2 + side],
                )
            )
    copy_all(copies)
    copy_all(pieces)

    @pl.when(encoder == 1)
    def _():
        pltpu.make_async_copy(
            context.at[core, :, pl.ds(first, RING * block)], base, sems.at[0]
        ).wait()

    @pl.when(encoder == 0)
    def _():
        pltpu.make_async_copy(
            queries.at[core, :, pl.ds(first, RING * block)],
            base.at[pl.ds(0, few)],
            sems.at[0],
        ).wait()

    wait_all(copies)
    for step in range(RING):
        wait_all(pieces[2 * step : 2 * step + 2])
        at = pl.ds(pl.multiple_of(((x - step + RING) % RING) * block, block), block)
        update = jnp.dot(heads[...], weight[step], preferred_element_type=F32)
        out[:, at] = (base[:, at].astype(F32) + update).astype(BF16)


def project(crossed, where, context, queries, mixed, weights):
    mem = context.shape[1]
    inner, block = weights[0].shape
    return call(
        functools.partial(project_kernel, crossed),
        jax.ShapeDtypeStruct((mem, RING * block), BF16),
        [SMEM] + [ANY] * 14,
        VMEM,
        [
            pltpu.VMEM((mem, 2 * inner), BF16),
            pltpu.VMEM((RING, 2 * inner, block), BF16),
            pltpu.VMEM((mem, RING * block), BF16),
            pltpu.SemaphoreType.DMA((17,)),
        ],
        flops=2 * mem * 2 * inner * RING * block,
        moved=2 * (2 * inner * RING * block + 3 * mem * inner),
    )(where, context, queries, *mixed, *weights)


def gather_kernel(where, *refs):
    near, far, ctx, qry = refs[0:2], refs[2:4], refs[4:6], refs[6:8]
    ctx_out, qry_out, sems = refs[8:]
    z, core, from_encoder = where[1], where[3], where[4]
    width = near[0].shape[1]
    few = qry[0].shape[0]

    @pl.when(from_encoder == 1)
    def _():
        copies = []
        for side in range(2):
            scene = core if side == 0 else 1 - core
            for i, (piece, half) in enumerate(((near, z), (far, 1 - z))):
                at = pl.ds(pl.multiple_of(half * width, width), width)
                copies.append(
                    pltpu.make_async_copy(
                        piece[side], ctx_out.at[scene, :, at], sems.at[3 * side + i]
                    )
                )
            copies.append(
                pltpu.make_async_copy(qry[side], qry_out.at[scene], sems.at[3 * side + 2])
            )
        wait_all(copy_all(copies))

    @pl.when(from_encoder == 0)
    def _():
        copies = []
        for side in range(2):
            scene = core if side == 0 else 1 - core
            for i, (piece, half) in enumerate(((near, z), (far, 1 - z))):
                at = pl.ds(pl.multiple_of(half * width, width), width)
                copies.append(
                    pltpu.make_async_copy(
                        piece[side].at[pl.ds(0, few)],
                        qry_out.at[scene, :, at],
                        sems.at[3 * side + i],
                    )
                )
            copies.append(
                pltpu.make_async_copy(ctx[side], ctx_out.at[scene], sems.at[3 * side + 2])
            )
        wait_all(copy_all(copies))


def gather_result(where, near, far, ctx, qry):
    mem, width = ctx[0].shape
    few = qry[0].shape[0]
    return call(
        gather_kernel,
        (
            jax.ShapeDtypeStruct((2, mem, width), BF16),
            jax.ShapeDtypeStruct((2, few, width), BF16),
        ),
        [SMEM] + [ANY] * 8,
        (ANY, ANY),
        [pltpu.SemaphoreType.DMA((6,))],
        moved=8 * mem * width,
    )(where, *near, *far, *ctx, *qry)


def per_device(context, queries, lengths, norm_gain, qkv_weight, out_weight):
    count = lax.axis_size("section")
    section = lax.axis_index("section")
    place = lax.axis_index("dp")
    core = lax.axis_index("tensor")
    encoders = list(range(count // 2))
    decoders = list(range(count // 2, count))
    before = (section + count - 1) % count
    where = jnp.stack(
        [
            place % RING,
            place // RING,
            (section < count // 2).astype(jnp.int32),
            core,
            (before < count // 2).astype(jnp.int32),
        ]
    ).astype(jnp.int32)
    context, queries = context[0], queries[0]

    own = quarters(where, jnp.swapaxes(qkv_weight[0], 0, 1))
    near = [own[0]] + [around_x(own[step], step) for step in range(1, RING)]
    far = [across_z(piece) for piece in near]
    near_both = near + [other_core(piece) for piece in near]
    far_both = far + [other_core(piece) for piece in far]

    ctx, qry, ctx_norm, qry_norm = norm_scene(where, context, queries, norm_gain)
    half = ctx_norm.shape[0] // 2
    ctx_norm_sent = after(ctx_norm, near[1], near[2], near[3])
    from_left = around_x(ctx_norm_sent, 1)
    from_right = around_x(ctx_norm_sent, -1)
    opposite = [around_x(from_left[:half], 1), around_x(from_right[half:], -1)]
    ctx_rows = [ctx_norm, from_left, *opposite, from_right]
    qry_rows = [qry_norm] + [around_x_of(qry_norm, step, decoders) for step in range(1, RING)]
    length = jnp.full((8, 128), lax.dynamic_index_in_dim(lengths[0], core, keepdims=False))
    all_lengths = jnp.stack(
        [length[0, 0]] + [around_x(length, step)[0, 0] for step in range(1, RING)]
    )

    shard = after(out_weight[0], from_left, from_right)
    out_near = [shard] + [around_x(shard, step) for step in range(1, RING)]
    out_near += [other_core(piece) for piece in out_near]
    shard = across_z(after(out_weight[0], *far))
    out_far = [shard] + [around_x(shard, step) for step in range(1, RING)]
    out_far += [other_core(piece) for piece in out_far]

    ctx_early = relay(after(ctx, *far), decoders, count)
    qry_early = relay(after(qry, *far), encoders, count)

    mixed = attend(where, all_lengths, ctx_rows, qry_rows, near_both, far_both)
    mixed = [mixed[0]] + [around_x(mixed[step], -step) for step in range(1, RING)]

    everyone = encoders + decoders
    result_near = project(False, where, context, queries, mixed, out_near)
    sent_near = relay(result_near, everyone, count)
    result_far = project(True, where, context, queries, mixed, out_far)
    sent_far = relay(result_far, everyone, count)
    ctx_new, qry_new = gather_result(
        where,
        (sent_near, other_core(sent_near)),
        (sent_far, other_core(sent_far)),
        (ctx_early, other_core(ctx_early)),
        (qry_early, other_core(qry_early)),
    )
    return ctx_new[None], qry_new[None]


def solution(mesh):
    return jax.shard_map(
        per_device,
        mesh=mesh,
        in_specs=(
            P("section", "dp", None, None),
            P("section", "dp", None, None),
            P("section", "dp"),
            P("section", None),
            P("section", "dp", None, "tensor"),
            P("section", "tensor", "dp"),
        ),
        out_specs=(P("section", "dp", None, None), P("section", "dp", None, None)),
        check_vma=False,
    )
```

time: 489 us -> 376 us (0.77)
  waiting for transfers between devices: 433 us -> 92.7 us
  starting transfers between devices: 2.82 us -> 151 us
  Pallas kernels: 0 us -> 117 us
  matrix products: 21.9 us -> 0 us
  between operations: 13.9 us -> 1.33 us
    all_gather x2 -> x0, waiting for transfers between devices: 344 us -> none  [the longest x1 253 us: per_device(): weight_rows = lax.all_gather(qkv_weight, 'dp', axis=1, tiled=True)]
    ppermute x2 -> x51, starting transfers between devices: 2.7 us -> 151 us  [the longest x20 52.9 us: other_core(): return lax.ppermute(array, 'tensor', [(0, 1), (1, 0)])]
    pallas_call x0 -> x6, Pallas kernels: none -> 117 us  [the longest x1 81.2 us: gather_result(): call(gather_kernel, (jax.ShapeDtypeStruct((2, mem, width), BF16), jax.Sha...]
    ppermute x2 -> x51, waiting for transfers between devices: 58.3 us -> 92.7 us  [the longest x5 38.5 us: across_z(): lax.ppermute(array, 'dp', [(d, (d + RING) % (2 * RING)) for d in range(2...]
    psum x1 -> x0, waiting for transfers between devices: 30.2 us -> none  [per_device(): lax.psum(update.astype(jnp.bfloat16), 'tensor').astype(jnp.float32)]
    dot_general x4 -> x0, matrix products: 21.9 us -> none  [the longest x1 12.1 us: per_device(): jnp.dot(flat_rows, weight_rows[0].reshape(row_count, 3 * local_width), pr...]
    convert_element_type x3 -> x0, other arithmetic: 4.98 us -> none  [the longest x1 2.8 us: per_device(): fresh = (widened + head_total).astype(jnp.bfloat16)]
  transfers between devices with their start and end apart: 5 -> 51, of which waited for: 4 -> 17; matrix products, arithmetic and copies ran while one was open for 4% -> 2% of each run, Pallas kernels for 0% -> 8%
where the time goes in v1:
time: 376 us
  starting transfers between devices  151 us (40%)
  Pallas kernels  117 us (31%)
  waiting for transfers between devices  92.7 us (25%)
  local copies, waits for them, and re-layouts  9.92 us (3%)
    pallas_call x1, Pallas kernels, gather_result(): call(gather_kernel, (jax.ShapeDtypeStruct((2, mem, width), BF16), jax.Sha...  81.2 us
    ppermute x20, starting transfers between devices, other_core(): return lax.ppermute(array, 'tensor', [(0, 1), (1, 0)])  52.9 us
    ppermute x5, waiting for transfers between devices, across_z(): lax.ppermute(array, 'dp', [(d, (d + RING) % (2 * RING)) for d in range(2...  38.5 us
    ppermute x19, starting transfers between devices, around_x(): return lax.ppermute(array, 'dp', pairs)  37.3 us
    ppermute x19, waiting for transfers between devices, around_x(): return lax.ppermute(array, 'dp', pairs)  34.4 us
    ppermute x4, starting transfers between devices, relay(): lax.ppermute(array, 'section', [(s, (s + 1) % count) for s in sections])  29.3 us
    ppermute x5, starting transfers between devices, across_z(): lax.ppermute(array, 'dp', [(d, (d + RING) % (2 * RING)) for d in range(2...  24.5 us
    pallas_call x1, Pallas kernels, attend(): call(attend_kernel, (out,) * RING, [SMEM, SMEM] + [ANY] * len(operands),...  16.4 us
  transfers between devices with their start and end apart: 51, of which 17 were waited for; matrix products, arithmetic and copies ran while one was open for 2% of the time, Pallas kernels for 8%

profile of v1, /device:TPU:17, one launch (start us, length us, event | category | flops | bytes accessed | tf_op | source)
XLA Modules:
  0.0 375.8 jit_solution(137714751523043727)
XLA Ops:
  1.3 4.7 %shard_map.77 = (bf16[256,2048]{1,0:T(8,128)(2,1)}, bf16[64,2048]{1,0:T(8,128)(2,1)}, bf16[256,2048]{1,0:T(8,128)(2,1)}, bf16[64,2048]{1,0:T(8,128)(2,1)}) custom-call(s32[5]{0:T(128)} %stack.34.where, bf16[2,256,2048]{2,1,0:T(8,128)(2,1)} %bitcast.18, bf16[2,64,2048]{2,1,0:T(8,128)(2,1)} %bitcast.21, f32[1,2048]{1,0:T(1,128)} %gain.1), custom_call_target="tpu_custom_call" | custom-call | bytes 3145728 | tf_op jit(solution)/shard_map/pallas_call | solution.py:123
  6.0 3.1 collective-permute-start.10
  9.2 2.8 shard_map.78
  11.9 1.2 collective-permute-start.3
  14.4 1.5 collective-permute-start.1
  16.0 1.9 collective-permute-start.2
  17.8 7.9 %collective-permute-done.1 = s32[8,128]{1,0:T(8,128)S(1)} collective-permute-done((s32[8,128]{1,0:T(8,128)S(1)}, s32[8,128]{1,0:T(8,128)S(1)}, u32[]{:S(2)}, u32[]{:S(2)}) %collective-permute-start.1) | collective-permute-done | bytes 4128 | tf_op jit(solution)/shard_map/ppermute | solution.py:25
  25.7 2.4 collective-permute-start.11
  28.2 2.5 collective-permute-start.4
  30.7 1.9 collective-permute-start.12
  32.7 0.9 collective-permute-start.5
  33.5 1.7 collective-permute-done.11.refs_7_
  36.0 6.9 %collective-permute-start.17 = (bf16[3,256,256]{2,1,0:T(8,128)(2,1)}, bf16[3,256,256]{2,1,0:T(8,128)(2,1)S(1)}, u32[]{:S(2)}, u32[]{:S(2)}) collective-permute-start(bf16[3,256,256]{2,1,0:T(8,128)(2,1)} %get-tuple-element.27.refs_9_), channel_id=1, source_target_pairs={{0,8},{2,10},{4,12},{6,14},{8,0},{10,2},{12,4},{14,6},{1,9},{3,11}... | collective-permute-start | bytes 1179656 | tf_op jit(solution)/shard_map/ppermute | solution.py:39
  42.9 5.5 %collective-permute-start.13 = (bf16[3,256,256]{2,1,0:T(8,128)(2,1)}, bf16[3,256,256]{2,1,0:T(8,128)(2,1)S(1)}, u32[]{:S(2)}, u32[]{:S(2)}) collective-permute-start(bf16[3,256,256]{2,1,0:T(8,128)(2,1)} %get-tuple-element.27.refs_9_), channel_id=1, source_target_pairs={{0,1},{1,0},{2,3},{3,2},{4,5},{5,4},{6,7},{7,6},{8,9},{9,8},{10,11... | collective-permute-start | bytes 1179656 | tf_op jit(solution)/shard_map/ppermute | solution.py:43
  48.4 5.7 %collective-permute-start.18 = (bf16[3,256,256]{2,1,0:T(8,128)(2,1)S(1)}, bf16[3,256,256]{2,1,0:T(8,128)(2,1)S(1)}, u32[]{:S(2)}, u32[]{:S(2)}) collective-permute-start(bf16[3,256,256]{2,1,0:T(8,128)(2,1)S(1)} %collective-permute-done.3.refs_10_), channel_id=1, source_target_pairs={{0,8},{2,10},{4,12},{6,14},{8,0},{10,2},{12,4},{14,6},{1,9},{3,11}... | collective-permute-start | bytes 1179656 | tf_op jit(solution)/shard_map/ppermute | solution.py:39
  54.3 5.3 %collective-permute-start.20 = (bf16[3,256,256]{2,1,0:T(8,128)(2,1)S(1)}, bf16[3,256,256]{2,1,0:T(8,128)(2,1)S(1)}, u32[]{:S(2)}, u32[]{:S(2)}) collective-permute-start(bf16[3,256,256]{2,1,0:T(8,128)(2,1)S(1)} %collective-permute-done.5.refs_12_), channel_id=1, source_target_pairs={{0,8},{2,10},{4,12},{6,14},{8,0},{10,2},{12,4},{14,6},{1,9},{3,11}... | collective-permute-start | bytes 1179656 | tf_op jit(solution)/shard_map/ppermute | solution.py:39
  59.6 0.9 collective-permute-start.14
  60.6 5.9 %collective-permute-done.18.refs_18_ = bf16[3,256,256]{2,1,0:T(8,128)(2,1)S(1)} collective-permute-done((bf16[3,256,256]{2,1,0:T(8,128)(2,1)S(1)}, bf16[3,256,256]{2,1,0:T(8,128)(2,1)S(1)}, u32[]{:S(2)}, u32[]{:S(2)}) %collective-permute-start.18) | collective-permute-done | bytes 393248 | tf_op jit(solution)/shard_map/ppermute | solution.py:39
  66.5 1.1 collective-permute-start.16
  67.6 10.6 %collective-permute-done.19.refs_19_ = bf16[3,256,256]{2,1,0:T(8,128)(2,1)S(1)} collective-permute-done((bf16[3,256,256]{2,1,0:T(8,128)(2,1)S(1)}, bf16[3,256,256]{2,1,0:T(8,128)(2,1)S(1)}, u32[]{:S(2)}, u32[]{:S(2)}) %collective-permute-start.19) | collective-permute-done | bytes 393248 | tf_op jit(solution)/shard_map/ppermute | solution.py:39
  78.2 1.0 collective-permute-start.21
  79.2 12.8 %collective-permute-done.20.refs_20_ = bf16[3,256,256]{2,1,0:T(8,128)(2,1)S(1)} collective-permute-done((bf16[3,256,256]{2,1,0:T(8,128)(2,1)S(1)}, bf16[3,256,256]{2,1,0:T(8,128)(2,1)S(1)}, u32[]{:S(2)}, u32[]{:S(2)}) %collective-permute-start.20) | collective-permute-done | bytes 393248 | tf_op jit(solution)/shard_map/ppermute | solution.py:39
  92.0 19.1 %collective-permute-start.22 = (bf16[3,256,256]{2,1,0:T(8,128)(2,1)S(1)}, bf16[3,256,256]{2,1,0:T(8,128)(2,1)S(1)}, u32[]{:S(2)}, u32[]{:S(2)}) collective-permute-start(bf16[3,256,256]{2,1,0:T(8,128)(2,1)S(1)} %collective-permute-done.18.refs_18_), channel_id=1, source_target_pairs={{0,1},{1,0},{2,3},{3,2},{4,5},{5,4},{6,7},{7,6},{8,9},{9,8},{10,11... | collective-permute-start | bytes 1179656 | tf_op jit(solution)/shard_map/ppermute | solution.py:43
  111.2 2.7 collective-permute-start.8
  113.9 6.4 %collective-permute-start.37 = (bf16[1024,256]{1,0:T(8,128)(2,1)S(1)}, bf16[1024,256]{1,0:T(8,128)(2,1)S(1)}, u32[]{:S(2)}, u32[]{:S(2)}) collective-permute-start(bf16[1024,256]{1,0:T(8,128)(2,1)S(1)} %bitcast.26), channel_id=1, source_target_pairs={{0,8},{2,10},{4,12},{6,14},{8,0},{10,2},{12,4},{14,6},{1,9},{3,11}... | collective-permute-start | bytes 1572872 | tf_op jit(solution)/shard_map/ppermute | solution.py:39
  120.3 0.9 collective-permute-start.23
  121.3 1.2 collective-permute-done.23.refs_23_
  122.5 3.1 collective-permute-start.47
  125.7 9.2 %collective-permute-done.37.refs_4_ = bf16[1024,256]{1,0:T(8,128)(2,1)S(1)} collective-permute-done((bf16[1024,256]{1,0:T(8,128)(2,1)S(1)}, bf16[1024,256]{1,0:T(8,128)(2,1)S(1)}, u32[]{:S(2)}, u32[]{:S(2)}) %collective-permute-start.37) | collective-permute-done | bytes 524320 | tf_op jit(solution)/shard_map/ppermute | solution.py:39
  134.9 8.3 %collective-permute-start.38 = (bf16[1024,256]{1,0:T(8,128)(2,1)S(1)}, bf16[1024,256]{1,0:T(8,128)(2,1)S(1)}, u32[]{:S(2)}, u32[]{:S(2)}) collective-permute-start(bf16[1024,256]{1,0:T(8,128)(2,1)S(1)} %collective-permute-done.37.refs_4_), channel_id=1, source_target_pairs={{0,2},{2,4},{4,6},{6,0},{8,10},{10,12},{12,14},{14,8},{1,3},{3,5},... | collective-permute-start | bytes 1572872 | tf_op jit(solution)/shard_map/ppermute | solution.py:25
  143.2 2.4 collective-permute-start.39
  145.6 2.1 collective-permute-start.40
  147.7 2.3 collective-permute-start.41
  150.2 2.3 collective-permute-done.38.refs_5_
  152.4 3.3 collective-permute-start.7
  155.7 11.8 %collective-permute-done.39.refs_6_ = bf16[1024,256]{1,0:T(8,128)(2,1)S(1)} collective-permute-done((bf16[1024,256]{1,0:T(8,128)(2,1)S(1)}, bf16[1024,256]{1,0:T(8,128)(2,1)S(1)}, u32[]{:S(2)}, u32[]{:S(2)}) %collective-permute-start.39) | collective-permute-done | bytes 524320 | tf_op jit(solution)/shard_map/ppermute | solution.py:25
  169.2 3.2 pad_add_fusion.lengths
  172.5 1.5 collective-permute-start.28
  174.1 2.4 collective-permute-start.30
  176.5 2.0 collective-permute-done.7.refs_2_
  178.4 2.6 collective-permute-start.42
  181.1 0.8 copy-done.31
  181.8 9.1 %collective-permute-start.43 = (bf16[1024,256]{1,0:T(8,128)(2,1)S(1)}, bf16[1024,256]{1,0:T(8,128)(2,1)S(1)}, u32[]{:S(2)}, u32[]{:S(2)}) collective-permute-start(bf16[1024,256]{1,0:T(8,128)(2,1)S(1)} %collective-permute-done.39.refs_6_), channel_id=1, source_target_pairs={{0,1},{1,0},{2,3},{3,2},{4,5},{5,4},{6,7},{7,6},{8,9},{9,8},{10,11... | collective-permute-start | bytes 1572872 | tf_op jit(solution)/shard_map/ppermute | solution.py:43
  191.0 16.4 %shard_map.79 = (bf16[256,512]{1,0:T(8,128)(2,1)}, bf16[256,512]{1,0:T(8,128)(2,1)}, bf16[256,512]{1,0:T(8,128)(2,1)}, bf16[256,512]{1,0:T(8,128)(2,1)}) custom-call(s32[5]{0:T(128)} %stack.34.where, s32[4]{0:T(128)} %pad_add_fusion.lengths, bf16[256,2048]{1,0:T(8,128)(2,1)} %get-tuple-element.25.refs_0_, bf16[256,2048]{1,0:T(8,128)(2,1)} %copy-done.28, ...), custom_call_target="tpu_custom_call" | custom-call | flops 6442450944 | bytes 10485760 | tf_op jit(solution)/shard_map/pallas_call | solution.py:229
  207.4 4.2 %collective-permute-start.25 = (bf16[256,512]{1,0:T(8,128)(2,1)}, bf16[256,512]{1,0:T(8,128)(2,1)S(1)}, u32[]{:S(2)}, u32[]{:S(2)}) collective-permute-start(bf16[256,512]{1,0:T(8,128)(2,1)} %get-tuple-element.29), channel_id=1, source_target_pairs={{0,6},{2,0},{4,2},{6,4},{8,14},{10,8},{12,10},{14,12},{1,7},{3,1},... | collective-permute-start | bytes 786440 | tf_op jit(solution)/shard_map/ppermute | solution.py:25
  211.7 2.3 collective-permute-start.26
  214.0 5.0 %collective-permute-done.25.refs_1_ = bf16[256,512]{1,0:T(8,128)(2,1)S(1)} collective-permute-done((bf16[256,512]{1,0:T(8,128)(2,1)}, bf16[256,512]{1,0:T(8,128)(2,1)S(1)}, u32[]{:S(2)}, u32[]{:S(2)}) %collective-permute-start.25) | collective-permute-done | bytes 262176 | tf_op jit(solution)/shard_map/ppermute | solution.py:25
  219.0 0.9 collective-permute-start.44
  219.9 1.1 collective-permute-done.26.refs_2_
  221.0 1.9 collective-permute-start.31
  222.9 4.3 %collective-permute-done.27.refs_3_ = bf16[256,512]{1,0:T(8,128)(2,1)S(1)} collective-permute-done((bf16[256,512]{1,0:T(8,128)(2,1)}, bf16[256,512]{1,0:T(8,128)(2,1)S(1)}, u32[]{:S(2)}, u32[]{:S(2)}) %collective-permute-start.27) | collective-permute-done | bytes 262176 | tf_op jit(solution)/shard_map/ppermute | solution.py:25
  229.5 6.0 %shard_map.81 = bf16[256,1024]{1,0:T(8,128)(2,1)} custom-call(s32[5]{0:T(128)} %stack.34.where, bf16[2,256,2048]{2,1,0:T(8,128)(2,1)} %bitcast.19, bf16[2,64,2048]{2,1,0:T(8,128)(2,1)} %bitcast.22, bf16[256,512]{1,0:T(8,128)(2,1)} %get-tuple-element.28.refs_0_, bf16[256,512]{1,0:T(8,128)(2,1)} %copy-done.3, bf16[256,512]{1,0:T(8,128)(2,1)} %copy-done.4, ...), custom_call_target="tpu_custom_call" | custom-call | flops 1073741824 | bytes 5767168 | tf_op jit(solution)/shard_map/pallas_call | solution.py:324
  235.6 24.8 %collective-permute-start.45 = (bf16[256,1024]{1,0:T(8,128)(2,1)}, bf16[256,1024]{1,0:T(8,128)(2,1)S(1)}, u32[]{:S(2)}, u32[]{:S(2)}) collective-permute-start(bf16[256,1024]{1,0:T(8,128)(2,1)} %shard_map.81), channel_id=1, source_target_pairs={{0,16},{16,32},{32,48},{48,64},{64,80},{80,96},{96,112},{112,128},... | collective-permute-start | bytes 1572872 | tf_op jit(solution)/shard_map/ppermute | solution.py:47
  262.2 6.0 %shard_map.80 = bf16[256,1024]{1,0:T(8,128)(2,1)} custom-call(s32[5]{0:T(128)} %stack.34.where, bf16[2,256,2048]{2,1,0:T(8,128)(2,1)} %bitcast.20, bf16[2,64,2048]{2,1,0:T(8,128)(2,1)} %bitcast.23, bf16[256,512]{1,0:T(8,128)(2,1)} %get-tuple-element.28.refs_0_, bf16[256,512]{1,0:T(8,128)(2,1)} %copy-done.3, bf16[256,512]{1,0:T(8,128)(2,1)} %copy-done.4, ...), custom_call_target="tpu_custom_call" | custom-call | flops 1073741824 | bytes 5767168 | tf_op jit(solution)/shard_map/pallas_call | solution.py:324
  268.4 1.3 collective-permute-start.49
  269.7 2.0 collective-permute-done.45.refs_2_
  271.7 1.9 collective-permute-start.46
  273.6 10.5 %collective-permute-done.35.refs_0_ = bf16[256,1024]{1,0:T(8,128)(2,1)S(1)} collective-permute-done((bf16[256,1024]{1,0:T(8,128)(2,1)}, bf16[256,1024]{1,0:T(8,128)(2,1)S(1)}, u32[]{:S(2)}, u32[]{:S(2)}) %collective-permute-start.35) | collective-permute-done | bytes 524320 | tf_op jit(solution)/shard_map/ppermute | solution.py:47
  284.1 2.5 collective-permute-start.36
  286.6 3.1 collective-permute-done.49.refs_6_
  289.7 1.5 collective-permute-start.50
  291.2 1.2 collective-permute-done.50.refs_7_
  293.6 0.8 copy-done.25
  294.4 81.2 %shard_map.82 = (bf16[2,256,2048]{2,1,0:T(8,128)(2,1)}, bf16[2,64,2048]{2,1,0:T(8,128)(2,1)}) custom-call(s32[5]{0:T(128)} %stack.34.where, bf16[256,1024]{1,0:T(8,128)(2,1)} %copy-done.21, bf16[256,1024]{1,0:T(8,128)(2,1)} %copy-done.25, bf16[256,1024]{1,0:T(8,128)(2,1)} %copy-done.17, bf16[256,1024]{1,0:T(8,128)(2,1)} %copy-done.24, ...), custom_call_target="tpu_custom_call" | custom-call | bytes 4194304 | tf_op jit(solution)/shard_map/pallas_call | solution.py:387
  (151 shorter events, 10.4 us)
Async XLA Ops:
  1.3 112.5 %copy-start.6 = (bf16[1,1024,256]{2,1,0:T(8,128)(2,1)S(1)}, bf16[1,1024,256]{2,1,0:T(8,128)(2,1)}, u32[]{:S(2)}) copy-start(bf16[1,1024,256]{2,1,0:T(8,128)(2,1)} %param.11) | copy-start | bytes 1572868
  6.0 26.6 %collective-permute-start.10 = (bf16[64,2048]{1,0:T(8,128)(2,1)}, bf16[64,2048]{1,0:T(8,128)(2,1)S(1)}, u32[]{:S(2)}, u32[]{:S(2)}) collective-permute-start(bf16[64,2048]{1,0:T(8,128)(2,1)} %get-tuple-element.26.refs_5_), channel_id=1, source_target_pairs={{128,130},{130,132},{132,134},{134,128},{136,138},{138,140},{140,1... | collective-permute-start | bytes 786440 | tf_op jit(solution)/shard_map/ppermute | solution.py:35
  11.9 36.4 %collective-permute-start.3 = (bf16[3,256,256]{2,1,0:T(8,128)(2,1)}, bf16[3,256,256]{2,1,0:T(8,128)(2,1)S(1)}, u32[]{:S(2)}, u32[]{:S(2)}) collective-permute-start(bf16[3,256,256]{2,1,0:T(8,128)(2,1)} %get-tuple-element.22), channel_id=1, source_target_pairs={{0,2},{2,4},{4,6},{6,0},{8,10},{10,12},{12,14},{14,8},{1,3},{3,5},... | collective-permute-start | bytes 1179656 | tf_op jit(solution)/shard_map/ppermute | solution.py:25
  14.4 11.3 %collective-permute-start.1 = (s32[8,128]{1,0:T(8,128)S(1)}, s32[8,128]{1,0:T(8,128)S(1)}, u32[]{:S(2)}, u32[]{:S(2)}) collective-permute-start(s32[8,128]{1,0:T(8,128)S(1)} %broadcast_in_dim.9), channel_id=1, source_target_pairs={{0,4},{2,6},{4,0},{6,2},{8,12},{10,14},{12,8},{14,10},{1,5},{3,7},... | collective-permute-start | bytes 12296 | tf_op jit(solution)/shard_map/ppermute | solution.py:25
  16.0 12.2 %collective-permute-start.2 = (s32[8,128]{1,0:T(8,128)S(1)}, s32[8,128]{1,0:T(8,128)S(1)}, u32[]{:S(2)}, u32[]{:S(2)}) collective-permute-start(s32[8,128]{1,0:T(8,128)S(1)} %broadcast_in_dim.9), channel_id=1, source_target_pairs={{0,6},{2,0},{4,2},{6,4},{8,14},{10,8},{12,10},{14,12},{1,7},{3,1},... | collective-permute-start | bytes 12296 | tf_op jit(solution)/shard_map/ppermute | solution.py:25
  17.8 12.9 %collective-permute-start = (s32[8,128]{1,0:T(8,128)S(1)}, s32[8,128]{1,0:T(8,128)S(1)}, u32[]{:S(2)}, u32[]{:S(2)}) collective-permute-start(s32[8,128]{1,0:T(8,128)S(1)} %broadcast_in_dim.9), channel_id=1, source_target_pairs={{0,2},{2,4},{4,6},{6,0},{8,10},{10,12},{12,14},{14,8},{1,3},{3,5},... | collective-permute-start | bytes 12296 | tf_op jit(solution)/shard_map/ppermute | solution.py:25
  25.7 9.5 %collective-permute-start.11 = (bf16[64,2048]{1,0:T(8,128)(2,1)}, bf16[64,2048]{1,0:T(8,128)(2,1)S(1)}, u32[]{:S(2)}, u32[]{:S(2)}) collective-permute-start(bf16[64,2048]{1,0:T(8,128)(2,1)} %get-tuple-element.26.refs_5_), channel_id=1, source_target_pairs={{128,132},{130,134},{132,128},{134,130},{136,140},{138,142},{140,1... | collective-permute-start | bytes 786440 | tf_op jit(solution)/shard_map/ppermute | solution.py:35
  28.2 25.9 %collective-permute-start.4 = (bf16[3,256,256]{2,1,0:T(8,128)(2,1)}, bf16[3,256,256]{2,1,0:T(8,128)(2,1)S(1)}, u32[]{:S(2)}, u32[]{:S(2)}) collective-permute-start(bf16[3,256,256]{2,1,0:T(8,128)(2,1)} %get-tuple-element.23), channel_id=1, source_target_pairs={{0,4},{2,6},{4,0},{6,2},{8,12},{10,14},{12,8},{14,10},{1,5},{3,7},... | collective-permute-start | bytes 1179656 | tf_op jit(solution)/shard_map/ppermute | solution.py:25
  30.7 12.2 %collective-permute-start.12 = (bf16[64,2048]{1,0:T(8,128)(2,1)}, bf16[64,2048]{1,0:T(8,128)(2,1)}, u32[]{:S(2)}, u32[]{:S(2)}) collective-permute-start(bf16[64,2048]{1,0:T(8,128)(2,1)} %get-tuple-element.26.refs_5_), channel_id=1, source_target_pairs={{128,134},{130,128},{132,130},{134,132},{136,142},{138,136},{140,1... | collective-permute-start | bytes 786440 | tf_op jit(solution)/shard_map/ppermute | solution.py:35
  32.7 21.6 %collective-permute-start.5 = (bf16[3,256,256]{2,1,0:T(8,128)(2,1)}, bf16[3,256,256]{2,1,0:T(8,128)(2,1)S(1)}, u32[]{:S(2)}, u32[]{:S(2)}) collective-permute-start(bf16[3,256,256]{2,1,0:T(8,128)(2,1)} %get-tuple-element.24), channel_id=1, source_target_pairs={{0,6},{2,0},{4,2},{6,4},{8,14},{10,8},{12,10},{14,12},{1,7},{3,1},... | collective-permute-start | bytes 1179656 | tf_op jit(solution)/shard_map/ppermute | solution.py:25
  36.0 23.6 %collective-permute-start.17 = (bf16[3,256,256]{2,1,0:T(8,128)(2,1)}, bf16[3,256,256]{2,1,0:T(8,128)(2,1)S(1)}, u32[]{:S(2)}, u32[]{:S(2)}) collective-permute-start(bf16[3,256,256]{2,1,0:T(8,128)(2,1)} %get-tuple-element.27.refs_9_), channel_id=1, source_target_pairs={{0,8},{2,10},{4,12},{6,14},{8,0},{10,2},{12,4},{14,6},{1,9},{3,11}... | collective-permute-start | bytes 1179656 | tf_op jit(solution)/shard_map/ppermute | solution.py:39
  42.9 17.6 %collective-permute-start.13 = (bf16[3,256,256]{2,1,0:T(8,128)(2,1)}, bf16[3,256,256]{2,1,0:T(8,128)(2,1)S(1)}, u32[]{:S(2)}, u32[]{:S(2)}) collective-permute-start(bf16[3,256,256]{2,1,0:T(8,128)(2,1)} %get-tuple-element.27.refs_9_), channel_id=1, source_target_pairs={{0,1},{1,0},{2,3},{3,2},{4,5},{5,4},{6,7},{7,6},{8,9},{9,8},{10,11... | collective-permute-start | bytes 1179656 | tf_op jit(solution)/shard_map/ppermute | solution.py:43
  48.4 142.6 %copy-start.32 = (bf16[3,256,256]{2,1,0:T(8,128)(2,1)}, bf16[3,256,256]{2,1,0:T(8,128)(2,1)S(1)}, u32[]{:S(2)}) copy-start(bf16[3,256,256]{2,1,0:T(8,128)(2,1)S(1)} %collective-permute-done.3.refs_10_) | copy-start | bytes 1179652
  48.4 18.1 %collective-permute-start.18 = (bf16[3,256,256]{2,1,0:T(8,128)(2,1)S(1)}, bf16[3,256,256]{2,1,0:T(8,128)(2,1)S(1)}, u32[]{:S(2)}, u32[]{:S(2)}) collective-permute-start(bf16[3,256,256]{2,1,0:T(8,128)(2,1)S(1)} %collective-permute-done.3.refs_10_), channel_id=1, source_target_pairs={{0,8},{2,10},{4,12},{6,14},{8,0},{10,2},{12,4},{14,6},{1,9},{3,11}... | collective-permute-start | bytes 1179656 | tf_op jit(solution)/shard_map/ppermute | solution.py:39
  54.1 59.7 %copy-start.33 = (bf16[3,256,256]{2,1,0:T(8,128)(2,1)}, bf16[3,256,256]{2,1,0:T(8,128)(2,1)S(1)}, u32[]{:S(2)}) copy-start(bf16[3,256,256]{2,1,0:T(8,128)(2,1)S(1)} %collective-permute-done.4.refs_11_) | copy-start | bytes 1179652
  54.1 24.1 %collective-permute-start.19 = (bf16[3,256,256]{2,1,0:T(8,128)(2,1)S(1)}, bf16[3,256,256]{2,1,0:T(8,128)(2,1)S(1)}, u32[]{:S(2)}, u32[]{:S(2)}) collective-permute-start(bf16[3,256,256]{2,1,0:T(8,128)(2,1)S(1)} %collective-permute-done.4.refs_11_), channel_id=1, source_target_pairs={{0,8},{2,10},{4,12},{6,14},{8,0},{10,2},{12,4},{14,6},{1,9},{3,11}... | collective-permute-start | bytes 1179656 | tf_op jit(solution)/shard_map/ppermute | solution.py:39
  54.2 59.6 %copy-start.34 = (bf16[3,256,256]{2,1,0:T(8,128)(2,1)}, bf16[3,256,256]{2,1,0:T(8,128)(2,1)S(1)}, u32[]{:S(2)}) copy-start(bf16[3,256,256]{2,1,0:T(8,128)(2,1)S(1)} %collective-permute-done.5.refs_12_) | copy-start | bytes 1179652
  54.3 37.7 %collective-permute-start.20 = (bf16[3,256,256]{2,1,0:T(8,128)(2,1)S(1)}, bf16[3,256,256]{2,1,0:T(8,128)(2,1)S(1)}, u32[]{:S(2)}, u32[]{:S(2)}) collective-permute-start(bf16[3,256,256]{2,1,0:T(8,128)(2,1)S(1)} %collective-permute-done.5.refs_12_), channel_id=1, source_target_pairs={{0,8},{2,10},{4,12},{6,14},{8,0},{10,2},{12,4},{14,6},{1,9},{3,11}... | collective-permute-start | bytes 1179656 | tf_op jit(solution)/shard_map/ppermute | solution.py:39
  59.6 66.0 %copy-start.35 = (bf16[3,256,256]{2,1,0:T(8,128)(2,1)}, bf16[3,256,256]{2,1,0:T(8,128)(2,1)S(1)}, u32[]{:S(2)}) copy-start(bf16[3,256,256]{2,1,0:T(8,128)(2,1)S(1)} %collective-permute-done.17.refs_17_) | copy-start | bytes 1179652
  59.6 51.5 %collective-permute-start.14 = (bf16[3,256,256]{2,1,0:T(8,128)(2,1)S(1)}, bf16[3,256,256]{2,1,0:T(8,128)(2,1)}, u32[]{:S(2)}, u32[]{:S(2)}) collective-permute-start(bf16[3,256,256]{2,1,0:T(8,128)(2,1)S(1)} %collective-permute-done.3.refs_10_), channel_id=1, source_target_pairs={{0,1},{1,0},{2,3},{3,2},{4,5},{5,4},{6,7},{7,6},{8,9},{9,8},{10,11... | collective-permute-start | bytes 1179656 | tf_op jit(solution)/shard_map/ppermute | solution.py:43
  60.5 65.1 %copy-start.36 = (bf16[3,256,256]{2,1,0:T(8,128)(2,1)}, bf16[3,256,256]{2,1,0:T(8,128)(2,1)S(1)}, u32[]{:S(2)}) copy-start(bf16[3,256,256]{2,1,0:T(8,128)(2,1)S(1)} %collective-permute-done.13.refs_13_) | copy-start | bytes 1179652
  60.5 50.6 %collective-permute-start.15 = (bf16[3,256,256]{2,1,0:T(8,128)(2,1)S(1)}, bf16[3,256,256]{2,1,0:T(8,128)(2,1)S(1)}, u32[]{:S(2)}, u32[]{:S(2)}) collective-permute-start(bf16[3,256,256]{2,1,0:T(8,128)(2,1)S(1)} %collective-permute-done.4.refs_11_), channel_id=1, source_target_pairs={{0,1},{1,0},{2,3},{3,2},{4,5},{5,4},{6,7},{7,6},{8,9},{9,8},{10,11... | collective-permute-start | bytes 1179656 | tf_op jit(solution)/shard_map/ppermute | solution.py:43
  66.5 76.7 %copy-start.37 = (bf16[3,256,256]{2,1,0:T(8,128)(2,1)}, bf16[3,256,256]{2,1,0:T(8,128)(2,1)S(1)}, u32[]{:S(2)}) copy-start(bf16[3,256,256]{2,1,0:T(8,128)(2,1)S(1)} %collective-permute-done.18.refs_18_) | copy-start | bytes 1179652
  66.5 47.3 %collective-permute-start.16 = (bf16[3,256,256]{2,1,0:T(8,128)(2,1)S(1)}, bf16[3,256,256]{2,1,0:T(8,128)(2,1)S(1)}, u32[]{:S(2)}, u32[]{:S(2)}) collective-permute-start(bf16[3,256,256]{2,1,0:T(8,128)(2,1)S(1)} %collective-permute-done.5.refs_12_), channel_id=1, source_target_pairs={{0,1},{1,0},{2,3},{3,2},{4,5},{5,4},{6,7},{7,6},{8,9},{9,8},{10,11... | collective-permute-start | bytes 1179656 | tf_op jit(solution)/shard_map/ppermute | solution.py:43
  78.2 67.3 %copy-start.38 = (bf16[3,256,256]{2,1,0:T(8,128)(2,1)}, bf16[3,256,256]{2,1,0:T(8,128)(2,1)S(1)}, u32[]{:S(2)}) copy-start(bf16[3,256,256]{2,1,0:T(8,128)(2,1)S(1)} %collective-permute-done.19.refs_19_) | copy-start | bytes 1179652
  78.2 42.0 %collective-permute-start.21 = (bf16[3,256,256]{2,1,0:T(8,128)(2,1)S(1)}, bf16[3,256,256]{2,1,0:T(8,128)(2,1)S(1)}, u32[]{:S(2)}, u32[]{:S(2)}) collective-permute-start(bf16[3,256,256]{2,1,0:T(8,128)(2,1)S(1)} %collective-permute-done.17.refs_17_), channel_id=1, source_target_pairs={{0,1},{1,0},{2,3},{3,2},{4,5},{5,4},{6,7},{7,6},{8,9},{9,8},{10,11... | collective-permute-start | bytes 1179656 | tf_op jit(solution)/shard_map/ppermute | solution.py:43
  92.0 55.7 %copy-start.39 = (bf16[3,256,256]{2,1,0:T(8,128)(2,1)}, bf16[3,256,256]{2,1,0:T(8,128)(2,1)S(1)}, u32[]{:S(2)}) copy-start(bf16[3,256,256]{2,1,0:T(8,128)(2,1)S(1)} %collective-permute-done.20.refs_20_) | copy-start | bytes 1179652
  92.0 29.2 %collective-permute-start.22 = (bf16[3,256,256]{2,1,0:T(8,128)(2,1)S(1)}, bf16[3,256,256]{2,1,0:T(8,128)(2,1)S(1)}, u32[]{:S(2)}, u32[]{:S(2)}) collective-permute-start(bf16[3,256,256]{2,1,0:T(8,128)(2,1)S(1)} %collective-permute-done.18.refs_18_), channel_id=1, source_target_pairs={{0,1},{1,0},{2,3},{3,2},{4,5},{5,4},{6,7},{7,6},{8,9},{9,8},{10,11... | collective-permute-start | bytes 1179656 | tf_op jit(solution)/shard_map/ppermute | solution.py:43
  111.1 34.4 %collective-permute-start.6 = (bf16[256,2048]{1,0:T(8,128)(2,1)}, bf16[256,2048]{1,0:T(8,128)(2,1)S(1)}, u32[]{:S(2)}, u32[]{:S(2)}) collective-permute-start(bf16[256,2048]{1,0:T(8,128)(2,1)} %get-tuple-element.25.refs_0_), channel_id=1, source_target_pairs={{0,2},{2,4},{4,6},{6,0},{8,10},{10,12},{12,14},{14,8},{1,3},{3,5},... | collective-permute-start | bytes 3145736 | tf_op jit(solution)/shard_map/ppermute | solution.py:25
  111.2 36.5 %collective-permute-start.8 = (bf16[256,2048]{1,0:T(8,128)(2,1)}, bf16[256,2048]{1,0:T(8,128)(2,1)S(1)}, u32[]{:S(2)}, u32[]{:S(2)}) collective-permute-start(bf16[256,2048]{1,0:T(8,128)(2,1)} %get-tuple-element.25.refs_0_), channel_id=1, source_target_pairs={{0,6},{2,0},{4,2},{6,4},{8,14},{10,8},{12,10},{14,12},{1,7},{3,1},... | collective-permute-start | bytes 3145736 | tf_op jit(solution)/shard_map/ppermute | solution.py:25
  113.9 21.0 %collective-permute-start.37 = (bf16[1024,256]{1,0:T(8,128)(2,1)S(1)}, bf16[1024,256]{1,0:T(8,128)(2,1)S(1)}, u32[]{:S(2)}, u32[]{:S(2)}) collective-permute-start(bf16[1024,256]{1,0:T(8,128)(2,1)S(1)} %bitcast.26), channel_id=1, source_target_pairs={{0,8},{2,10},{4,12},{6,14},{8,0},{10,2},{12,4},{14,6},{1,9},{3,11}... | collective-permute-start | bytes 1572872 | tf_op jit(solution)/shard_map/ppermute | solution.py:39
  120.3 2.3 collective-permute-start.23
  121.2 22.0 %collective-permute-start.24 = (bf16[3,256,256]{2,1,0:T(8,128)(2,1)S(1)}, bf16[3,256,256]{2,1,0:T(8,128)(2,1)S(1)}, u32[]{:S(2)}, u32[]{:S(2)}) collective-permute-start(bf16[3,256,256]{2,1,0:T(8,128)(2,1)S(1)} %collective-permute-done.20.refs_20_), channel_id=1, source_target_pairs={{0,1},{1,0},{2,3},{3,2},{4,5},{5,4},{6,7},{7,6},{8,9},{9,8},{10,11... | collective-permute-start | bytes 1179656 | tf_op jit(solution)/shard_map/ppermute | solution.py:43
  122.5 51.5 %collective-permute-start.47 = (bf16[256,2048]{1,0:T(8,128)(2,1)}, bf16[256,2048]{1,0:T(8,128)(2,1)S(1)}, u32[]{:S(2)}, u32[]{:S(2)}) collective-permute-start(bf16[256,2048]{1,0:T(8,128)(2,1)} %get-tuple-element.35), channel_id=1, source_target_pairs={{128,144},{144,160},{160,176},{176,192},{192,208},{208,224},{224,2... | collective-permute-start | bytes 3145736 | tf_op jit(solution)/shard_map/ppermute | solution.py:47
  134.8 72.5 %copy-start.7 = (bf16[1024,256]{1,0:T(8,128)(2,1)}, bf16[1024,256]{1,0:T(8,128)(2,1)S(1)}, u32[]{:S(2)}) copy-start(bf16[1024,256]{1,0:T(8,128)(2,1)S(1)} %collective-permute-done.37.refs_4_) | copy-start | bytes 1572868
  134.9 17.6 %collective-permute-start.38 = (bf16[1024,256]{1,0:T(8,128)(2,1)S(1)}, bf16[1024,256]{1,0:T(8,128)(2,1)S(1)}, u32[]{:S(2)}, u32[]{:S(2)}) collective-permute-start(bf16[1024,256]{1,0:T(8,128)(2,1)S(1)} %collective-permute-done.37.refs_4_), channel_id=1, source_target_pairs={{0,2},{2,4},{4,6},{6,0},{8,10},{10,12},{12,14},{14,8},{1,3},{3,5},... | collective-permute-start | bytes 1572872 | tf_op jit(solution)/shard_map/ppermute | solution.py:25
  143.2 24.4 %collective-permute-start.39 = (bf16[1024,256]{1,0:T(8,128)(2,1)S(1)}, bf16[1024,256]{1,0:T(8,128)(2,1)S(1)}, u32[]{:S(2)}, u32[]{:S(2)}) collective-permute-start(bf16[1024,256]{1,0:T(8,128)(2,1)S(1)} %collective-permute-done.37.refs_4_), channel_id=1, source_target_pairs={{0,4},{2,6},{4,0},{6,2},{8,12},{10,14},{12,8},{14,10},{1,5},{3,7},... | collective-permute-start | bytes 1572872 | tf_op jit(solution)/shard_map/ppermute | solution.py:25
  145.6 26.9 %collective-permute-start.40 = (bf16[1024,256]{1,0:T(8,128)(2,1)S(1)}, bf16[1024,256]{1,0:T(8,128)(2,1)S(1)}, u32[]{:S(2)}, u32[]{:S(2)}) collective-permute-start(bf16[1024,256]{1,0:T(8,128)(2,1)S(1)} %collective-permute-done.37.refs_4_), channel_id=1, source_target_pairs={{0,6},{2,0},{4,2},{6,4},{8,14},{10,8},{12,10},{14,12},{1,7},{3,1},... | collective-permute-start | bytes 1572872 | tf_op jit(solution)/shard_map/ppermute | solution.py:25
  147.7 26.2 %collective-permute-start.41 = (bf16[1024,256]{1,0:T(8,128)(2,1)S(1)}, bf16[1024,256]{1,0:T(8,128)(2,1)S(1)}, u32[]{:S(2)}, u32[]{:S(2)}) collective-permute-start(bf16[1024,256]{1,0:T(8,128)(2,1)S(1)} %collective-permute-done.37.refs_4_), channel_id=1, source_target_pairs={{0,1},{1,0},{2,3},{3,2},{4,5},{5,4},{6,7},{7,6},{8,9},{9,8},{10,11... | collective-permute-start | bytes 1572872 | tf_op jit(solution)/shard_map/ppermute | solution.py:43
  152.4 55.0 %copy-start.8 = (bf16[1024,256]{1,0:T(8,128)(2,1)}, bf16[1024,256]{1,0:T(8,128)(2,1)S(1)}, u32[]{:S(2)}) copy-start(bf16[1024,256]{1,0:T(8,128)(2,1)S(1)} %collective-permute-done.38.refs_5_) | copy-start | bytes 1572868
  152.4 26.0 %collective-permute-start.7 = (bf16[128,2048]{1,0:T(8,128)(2,1)S(1)}, bf16[128,2048]{1,0:T(8,128)(2,1)S(1)}, u32[]{:S(2)}, u32[]{:S(2)}) collective-permute-start(bf16[128,2048]{1,0:T(8,128)(2,1)S(1)} %slice.21), channel_id=1, source_target_pairs={{0,2},{2,4},{4,6},{6,0},{8,10},{10,12},{12,14},{14,8},{1,3},{3,5},... | collective-permute-start | bytes 1572872 | tf_op jit(solution)/shard_map/ppermute | solution.py:25
  167.5 13.5 %collective-permute-start.9 = (bf16[128,2048]{1,0:T(8,128)(2,1)S(1)}, bf16[128,2048]{1,0:T(8,128)(2,1)S(1)}, u32[]{:S(2)}, u32[]{:S(2)}) collective-permute-start(bf16[128,2048]{1,0:T(8,128)(2,1)S(1)} %slice.22), channel_id=1, source_target_pairs={{0,6},{2,0},{4,2},{6,4},{8,14},{10,8},{12,10},{14,12},{1,7},{3,1},... | collective-permute-start | bytes 1572872 | tf_op jit(solution)/shard_map/ppermute | solution.py:25
  172.5 35.0 %collective-permute-start.28 = (bf16[1024,256]{1,0:T(8,128)(2,1)S(1)}, bf16[1024,256]{1,0:T(8,128)(2,1)S(1)}, u32[]{:S(2)}, u32[]{:S(2)}) collective-permute-start(bf16[1024,256]{1,0:T(8,128)(2,1)S(1)} %bitcast.27), channel_id=1, source_target_pairs={{0,2},{2,4},{4,6},{6,0},{8,10},{10,12},{12,14},{14,8},{1,3},{3,5},... | collective-permute-start | bytes 1572872 | tf_op jit(solution)/shard_map/ppermute | solution.py:25
  174.0 37.7 %collective-permute-start.29 = (bf16[1024,256]{1,0:T(8,128)(2,1)S(1)}, bf16[1024,256]{1,0:T(8,128)(2,1)S(1)}, u32[]{:S(2)}, u32[]{:S(2)}) collective-permute-start(bf16[1024,256]{1,0:T(8,128)(2,1)S(1)} %bitcast.28), channel_id=1, source_target_pairs={{0,4},{2,6},{4,0},{6,2},{8,12},{10,14},{12,8},{14,10},{1,5},{3,7},... | collective-permute-start | bytes 1572872 | tf_op jit(solution)/shard_map/ppermute | solution.py:25
  174.1 54.6 %copy-start.1 = (bf16[256,2048]{1,0:T(8,128)(2,1)}, bf16[256,2048]{1,0:T(8,128)(2,1)S(1)}, u32[]{:S(2)}) copy-start(bf16[256,2048]{1,0:T(8,128)(2,1)S(1)} %collective-permute-done.47.refs_4_) | copy-start | bytes 3145732
  174.1 39.9 %collective-permute-start.30 = (bf16[1024,256]{1,0:T(8,128)(2,1)S(1)}, bf16[1024,256]{1,0:T(8,128)(2,1)S(1)}, u32[]{:S(2)}, u32[]{:S(2)}) collective-permute-start(bf16[1024,256]{1,0:T(8,128)(2,1)S(1)} %bitcast.29), channel_id=1, source_target_pairs={{0,6},{2,0},{4,2},{6,4},{8,14},{10,8},{12,10},{14,12},{1,7},{3,1},... | collective-permute-start | bytes 1572872 | tf_op jit(solution)/shard_map/ppermute | solution.py:25
  178.4 49.3 %collective-permute-start.42 = (bf16[1024,256]{1,0:T(8,128)(2,1)S(1)}, bf16[1024,256]{1,0:T(8,128)(2,1)S(1)}, u32[]{:S(2)}, u32[]{:S(2)}) collective-permute-start(bf16[1024,256]{1,0:T(8,128)(2,1)S(1)} %collective-permute-done.38.refs_5_), channel_id=1, source_target_pairs={{0,1},{1,0},{2,3},{3,2},{4,5},{5,4},{6,7},{7,6},{8,9},{9,8},{10,11... | collective-permute-start | bytes 1572872 | tf_op jit(solution)/shard_map/ppermute | solution.py:43
  181.8 46.0 %collective-permute-start.43 = (bf16[1024,256]{1,0:T(8,128)(2,1)S(1)}, bf16[1024,256]{1,0:T(8,128)(2,1)S(1)}, u32[]{:S(2)}, u32[]{:S(2)}) collective-permute-start(bf16[1024,256]{1,0:T(8,128)(2,1)S(1)} %collective-permute-done.39.refs_6_), channel_id=1, source_target_pairs={{0,1},{1,0},{2,3},{3,2},{4,5},{5,4},{6,7},{7,6},{8,9},{9,8},{10,11... | collective-permute-start | bytes 1572872 | tf_op jit(solution)/shard_map/ppermute | solution.py:43
  207.4 53.0 %copy-start.12 = (bf16[1024,256]{1,0:T(8,128)(2,1)}, bf16[1024,256]{1,0:T(8,128)(2,1)S(1)}, u32[]{:S(2)}) copy-start(bf16[1024,256]{1,0:T(8,128)(2,1)S(1)} %collective-permute-done.28.refs_5_) | copy-start | bytes 1572868
  207.4 11.6 %collective-permute-start.25 = (bf16[256,512]{1,0:T(8,128)(2,1)}, bf16[256,512]{1,0:T(8,128)(2,1)S(1)}, u32[]{:S(2)}, u32[]{:S(2)}) collective-permute-start(bf16[256,512]{1,0:T(8,128)(2,1)} %get-tuple-element.29), channel_id=1, source_target_pairs={{0,6},{2,0},{4,2},{6,4},{8,14},{10,8},{12,10},{14,12},{1,7},{3,1},... | collective-permute-start | bytes 786440 | tf_op jit(solution)/shard_map/ppermute | solution.py:25
  211.7 9.3 %collective-permute-start.26 = (bf16[256,512]{1,0:T(8,128)(2,1)}, bf16[256,512]{1,0:T(8,128)(2,1)S(1)}, u32[]{:S(2)}, u32[]{:S(2)}) collective-permute-start(bf16[256,512]{1,0:T(8,128)(2,1)} %get-tuple-element.30), channel_id=1, source_target_pairs={{0,4},{2,6},{4,0},{6,2},{8,12},{10,14},{12,8},{14,10},{1,5},{3,7},... | collective-permute-start | bytes 786440 | tf_op jit(solution)/shard_map/ppermute | solution.py:25
  214.0 13.2 %collective-permute-start.27 = (bf16[256,512]{1,0:T(8,128)(2,1)}, bf16[256,512]{1,0:T(8,128)(2,1)S(1)}, u32[]{:S(2)}, u32[]{:S(2)}) collective-permute-start(bf16[256,512]{1,0:T(8,128)(2,1)} %get-tuple-element.31), channel_id=1, source_target_pairs={{0,2},{2,4},{4,6},{6,0},{8,10},{10,12},{12,14},{14,8},{1,3},{3,5},... | collective-permute-start | bytes 786440 | tf_op jit(solution)/shard_map/ppermute | solution.py:25
  219.0 9.7 %collective-permute-start.44 = (bf16[1024,256]{1,0:T(8,128)(2,1)S(1)}, bf16[1024,256]{1,0:T(8,128)(2,1)S(1)}, u32[]{:S(2)}, u32[]{:S(2)}) collective-permute-start(bf16[1024,256]{1,0:T(8,128)(2,1)S(1)} %collective-permute-done.40.refs_7_), channel_id=1, source_target_pairs={{0,1},{1,0},{2,3},{3,2},{4,5},{5,4},{6,7},{7,6},{8,9},{9,8},{10,11... | collective-permute-start | bytes 1572872 | tf_op jit(solution)/shard_map/ppermute | solution.py:43
  221.0 14.6 %collective-permute-start.31 = (bf16[1024,256]{1,0:T(8,128)(2,1)S(1)}, bf16[1024,256]{1,0:T(8,128)(2,1)S(1)}, u32[]{:S(2)}, u32[]{:S(2)}) collective-permute-start(bf16[1024,256]{1,0:T(8,128)(2,1)S(1)} %bitcast.30), channel_id=1, source_target_pairs={{0,1},{1,0},{2,3},{3,2},{4,5},{5,4},{6,7},{7,6},{8,9},{9,8},{10,11... | collective-permute-start | bytes 1572872 | tf_op jit(solution)/shard_map/ppermute | solution.py:43
  227.2 33.2 %collective-permute-start.32 = (bf16[1024,256]{1,0:T(8,128)(2,1)S(1)}, bf16[1024,256]{1,0:T(8,128)(2,1)S(1)}, u32[]{:S(2)}, u32[]{:S(2)}) collective-permute-start(bf16[1024,256]{1,0:T(8,128)(2,1)S(1)} %collective-permute-done.28.refs_5_), channel_id=1, source_target_pairs={{0,1},{1,0},{2,3},{3,2},{4,5},{5,4},{6,7},{7,6},{8,9},{9,8},{10,11... | collective-permute-start | bytes 1572872 | tf_op jit(solution)/shard_map/ppermute | solution.py:43
  227.7 32.7 %collective-permute-start.33 = (bf16[1024,256]{1,0:T(8,128)(2,1)S(1)}, bf16[1024,256]{1,0:T(8,128)(2,1)S(1)}, u32[]{:S(2)}, u32[]{:S(2)}) collective-permute-start(bf16[1024,256]{1,0:T(8,128)(2,1)S(1)} %collective-permute-done.29.refs_6_), channel_id=1, source_target_pairs={{0,1},{1,0},{2,3},{3,2},{4,5},{5,4},{6,7},{7,6},{8,9},{9,8},{10,11... | collective-permute-start | bytes 1572872 | tf_op jit(solution)/shard_map/ppermute | solution.py:43
  227.8 32.6 %collective-permute-start.34 = (bf16[1024,256]{1,0:T(8,128)(2,1)S(1)}, bf16[1024,256]{1,0:T(8,128)(2,1)S(1)}, u32[]{:S(2)}, u32[]{:S(2)}) collective-permute-start(bf16[1024,256]{1,0:T(8,128)(2,1)S(1)} %collective-permute-done.30.refs_7_), channel_id=1, source_target_pairs={{0,1},{1,0},{2,3},{3,2},{4,5},{5,4},{6,7},{7,6},{8,9},{9,8},{10,11... | collective-permute-start | bytes 1572872 | tf_op jit(solution)/shard_map/ppermute | solution.py:43
  228.7 63.6 %collective-permute-start.48 = (bf16[256,2048]{1,0:T(8,128)(2,1)S(1)}, bf16[256,2048]{1,0:T(8,128)(2,1)S(1)}, u32[]{:S(2)}, u32[]{:S(2)}) collective-permute-start(bf16[256,2048]{1,0:T(8,128)(2,1)S(1)} %collective-permute-done.47.refs_4_), channel_id=1, source_target_pairs={{0,1},{1,0},{2,3},{3,2},{4,5},{5,4},{6,7},{7,6},{8,9},{9,8},{10,11... | collective-permute-start | bytes 3145736 | tf_op jit(solution)/shard_map/ppermute | solution.py:43
  235.6 36.1 %collective-permute-start.45 = (bf16[256,1024]{1,0:T(8,128)(2,1)}, bf16[256,1024]{1,0:T(8,128)(2,1)S(1)}, u32[]{:S(2)}, u32[]{:S(2)}) collective-permute-start(bf16[256,1024]{1,0:T(8,128)(2,1)} %shard_map.81), channel_id=1, source_target_pairs={{0,16},{16,32},{32,48},{48,64},{64,80},{80,96},{96,112},{112,128},... | collective-permute-start | bytes 1572872 | tf_op jit(solution)/shard_map/ppermute | solution.py:47
  268.2 15.9 %collective-permute-start.35 = (bf16[256,1024]{1,0:T(8,128)(2,1)}, bf16[256,1024]{1,0:T(8,128)(2,1)S(1)}, u32[]{:S(2)}, u32[]{:S(2)}) collective-permute-start(bf16[256,1024]{1,0:T(8,128)(2,1)} %shard_map.80), channel_id=1, source_target_pairs={{0,16},{16,32},{32,48},{48,64},{64,80},{80,96},{96,112},{112,128},... | collective-permute-start | bytes 1572872 | tf_op jit(solution)/shard_map/ppermute | solution.py:47
  268.4 21.3 %collective-permute-start.49 = (bf16[64,2048]{1,0:T(8,128)(2,1)S(1)}, bf16[64,2048]{1,0:T(8,128)(2,1)S(1)}, u32[]{:S(2)}, u32[]{:S(2)}) collective-permute-start(bf16[64,2048]{1,0:T(8,128)(2,1)S(1)} %copy-done.46), channel_id=1, source_target_pairs={{0,16},{16,32},{32,48},{48,64},{64,80},{80,96},{96,112},{112,128},... | collective-permute-start | bytes 786440 | tf_op jit(solution)/shard_map/ppermute | solution.py:47
  271.7 20.7 %collective-permute-start.46 = (bf16[256,1024]{1,0:T(8,128)(2,1)S(1)}, bf16[256,1024]{1,0:T(8,128)(2,1)S(1)}, u32[]{:S(2)}, u32[]{:S(2)}) collective-permute-start(bf16[256,1024]{1,0:T(8,128)(2,1)S(1)} %collective-permute-done.45.refs_2_), channel_id=1, source_target_pairs={{0,1},{1,0},{2,3},{3,2},{4,5},{5,4},{6,7},{7,6},{8,9},{9,8},{10,11... | collective-permute-start | bytes 1572872 | tf_op jit(solution)/shard_map/ppermute | solution.py:43
  284.1 8.3 %collective-permute-start.36 = (bf16[256,1024]{1,0:T(8,128)(2,1)S(1)}, bf16[256,1024]{1,0:T(8,128)(2,1)S(1)}, u32[]{:S(2)}, u32[]{:S(2)}) collective-permute-start(bf16[256,1024]{1,0:T(8,128)(2,1)S(1)} %collective-permute-done.35.refs_0_), channel_id=1, source_target_pairs={{0,1},{1,0},{2,3},{3,2},{4,5},{5,4},{6,7},{7,6},{8,9},{9,8},{10,11... | collective-permute-start | bytes 1572872 | tf_op jit(solution)/shard_map/ppermute | solution.py:43
  289.7 2.6 collective-permute-start.50
  (36 other events, 649.7 us)
